TPU v7x, 512 devices: a whole 4x8x8 slice. The times are simulated.
512 devices in a mesh: tm: 32 (over y_lo, z), fsdp: 16 (over x, y_hi, core).
Axes of the slice: x: 4, y: 8 (y_hi: 2, y_lo: 4; y = y_hi * 4 + y_lo), z: 8, core: 2. Of those that a mesh axis runs over, the one named last changes fastest.
Arguments:
- queries: bfloat16 [128, 512, 12, 128], P('tm', 'fsdp'), may hold values from -5 to 5
- key_states: bfloat16 [128, 512, 12, 128], P('tm', 'fsdp'), may hold values from -5 to 5
- value_states: bfloat16 [128, 512, 12, 128], P('tm', 'fsdp'), may hold values from -6 to 6
- out_grad: bfloat16 [128, 512, 3072], P('tm', 'fsdp'), may hold values from -6 to 6
- out_proj: bfloat16 [1536, 3072], P('fsdp'), may hold values from -0.109375 to 0.109375
Outputs:
- query_grad: bfloat16 [128, 512, 12, 128], P('tm', 'fsdp')
- key_grad: bfloat16 [128, 512, 12, 128], P('tm', 'fsdp')
- value_grad: bfloat16 [128, 512, 12, 128], P('tm', 'fsdp')
All inputs are finite; a program needn't handle non-finite values.
Results may differ from a plain program's by a relative error of at most 0.03.
Values may be sent and summed in bfloat16 or wider, within the bound.
A program may use at most 64 MiB of HBM per device.

v0:
```python
import jax
import jax.numpy as jnp
from jax import lax
from jax.sharding import PartitionSpec as P


def attend_back(query_block, key_block, value_block, grad_block):
    score_scale = query_block.shape[-1] ** (-0.5)
    scores = (
        jnp.einsum("fphd,gphd->phfg", query_block, key_block, preferred_element_type=jnp.float32)
        * score_scale
    )
    peak = jnp.max(scores, axis=-1, keepdims=True)
    expo = jnp.exp(scores - peak)
    probs = expo / jnp.sum(expo, axis=-1, keepdims=True)
    probs_b = probs.astype(jnp.bfloat16)
    attn_out = jnp.einsum(
        "phfg,gphd->fphd", probs_b, value_block, preferred_element_type=jnp.float32
    )
    row_delta = jnp.einsum("fphd,fphd->phf", grad_block.astype(jnp.float32), attn_out)
    dprobs = jnp.einsum(
        "fphd,gphd->phfg", grad_block, value_block, preferred_element_type=jnp.float32
    )
    dscores = (probs * (dprobs - row_delta[..., None])).astype(jnp.bfloat16)
    query_grad = (
        jnp.einsum("phfg,gphd->fphd", dscores, key_block, preferred_element_type=jnp.float32)
        * score_scale
    ).astype(jnp.bfloat16)
    key_grad = (
        jnp.einsum("phfg,fphd->gphd", dscores, query_block, preferred_element_type=jnp.float32)
        * score_scale
    ).astype(jnp.bfloat16)
    value_grad = jnp.einsum(
        "phfg,fphd->gphd", probs_b, grad_block, preferred_element_type=jnp.float32
    ).astype(jnp.bfloat16)
    return (query_grad, key_grad, value_grad)


def send_back(grads):
    return (
        lax.all_to_all(grads[0], "tm", split_axis=0, concat_axis=1, tiled=True),
        lax.all_to_all(grads[1], "tm", split_axis=0, concat_axis=1, tiled=True),
        lax.all_to_all(grads[2], "tm", split_axis=0, concat_axis=1, tiled=True),
    )


def body(queries, key_states, value_states, out_grad, out_proj):
    frames_dev, pos_dev, heads, head_size = queries.shape
    width = out_grad.shape[-1]
    flat = out_grad.reshape(frames_dev * pos_dev, width)
    grad_flat = lax.dot_general(
        flat,
        lax.all_gather(out_proj, "fsdp", axis=0, tiled=True),
        (((1,), (1,)), ((), ())),
        preferred_element_type=jnp.float32,
    ).astype(jnp.bfloat16)
    grad_attn = grad_flat.reshape(frames_dev, pos_dev, heads, head_size)
    results = send_back(
        attend_back(
            lax.all_to_all(queries, "tm", split_axis=1, concat_axis=0, tiled=True),
            lax.all_to_all(key_states, "tm", split_axis=1, concat_axis=0, tiled=True),
            lax.all_to_all(value_states, "tm", split_axis=1, concat_axis=0, tiled=True),
            lax.all_to_all(grad_attn, "tm", split_axis=1, concat_axis=0, tiled=True),
        )
    )
    return (results[0], results[1], results[2])


def solution(mesh):
    return jax.shard_map(
        body,
        mesh=mesh,
        in_specs=(
            P("tm", "fsdp", None, None),
            P("tm", "fsdp", None, None),
            P("tm", "fsdp", None, None),
            P("tm", "fsdp", None),
            P("fsdp", None),
        ),
        out_specs=(
            P("tm", "fsdp", None, None),
            P("tm", "fsdp", None, None),
            P("tm", "fsdp", None, None),
        ),
        check_vma=False,
    )
```

profile of v0, /device:TPU:64, one launch (start us, length us, event | category | flops | bytes accessed | tf_op | source)
XLA Modules:
  0.0 255.6 jit_solution(9501734445395635205)
XLA Ops:
  7.2 0.7 all-gather.2.cloned.1.call-update
  7.9 2.0 copy.39
  9.9 13.2 %all-to-all-start = ((bf16[4,32,12,128]{3,2,0,1:T(8,128)(2,1)}), bf16[4,32,12,128]{3,2,0,1:T(8,128)(2,1)S(1)}, u32[]{:S(2)}, u32[]{:S(2)}) async-start(bf16[4,32,12,128]{3,2,0,1:T(8,128)(2,1)} %copy.39), calls=%async_computation | async-start | bytes 1048576 | tf_op jit(solution)/shard_map/all_to_all | solution.py:60
  23.1 2.0 copy.41
  25.0 22.8 %all-to-all-done = bf16[4,32,12,128]{3,2,0,1:T(8,128)(2,1)S(1)} async-done(((bf16[4,32,12,128]{3,2,0,1:T(8,128)(2,1)}), bf16[4,32,12,128]{3,2,0,1:T(8,128)(2,1)S(1)}, u32[]{:S(2)}, u32[]{:S(2)}) %all-to-all-start) | async-done | bytes 393248 | tf_op jit(solution)/shard_map/all_to_all | solution.py:60
  47.8 6.2 %all-to-all-start.1 = ((bf16[4,32,12,128]{3,2,0,1:T(8,128)(2,1)}), bf16[4,32,12,128]{3,2,0,1:T(8,128)(2,1)S(1)}, u32[]{:S(2)}, u32[]{:S(2)}) async-start(bf16[4,32,12,128]{3,2,0,1:T(8,128)(2,1)} %copy.41), calls=%async_computation.1 | async-start | bytes 1048576 | tf_op jit(solution)/shard_map/all_to_all | solution.py:61
  54.0 2.0 copy.45
  56.0 14.3 %all-to-all-done.1 = bf16[4,32,12,128]{3,2,0,1:T(8,128)(2,1)S(1)} async-done(((bf16[4,32,12,128]{3,2,0,1:T(8,128)(2,1)}), bf16[4,32,12,128]{3,2,0,1:T(8,128)(2,1)S(1)}, u32[]{:S(2)}, u32[]{:S(2)}) %all-to-all-start.1) | async-done | bytes 393248 | tf_op jit(solution)/shard_map/all_to_all | solution.py:61
  70.3 4.7 %all-to-all-start.3 = ((bf16[4,32,12,128]{3,2,0,1:T(8,128)(2,1)}), bf16[4,32,12,128]{3,2,0,1:T(8,128)(2,1)S(1)}, u32[]{:S(2)}, u32[]{:S(2)}) async-start(bf16[4,32,12,128]{3,2,0,1:T(8,128)(2,1)} %copy.45), calls=%async_computation.3 | async-start | bytes 1048576 | tf_op jit(solution)/shard_map/all_to_all | solution.py:62
  75.0 71.0 %all-gather.2.cloned.1.call-done = bf16[1536,3072]{1,0:T(8,128)(2,1)} async-done(((bf16[96,3072]{1,0:T(8,128)(2,1)}), bf16[1536,3072]{1,0:T(8,128)(2,1)}) %all-gather.2.cloned.1.call-update) | async-done | bytes 9437200 | tf_op jit(solution)/shard_map/all_gather | solution.py:53
  146.0 6.9 %convolution_convert_fusion = bf16[128,1536]{1,0:T(8,128)(2,1)S(1)} fusion(bf16[128,3072]{1,0:T(8,128)(2,1)S(1)} %bitcast.71, bf16[1536,3072]{1,0:T(8,128)(2,1)} %all-gather.2.cloned.1.call-done), kind=kOutput, calls=%fused_computation.1 | convolution fusion | flops 1208156160 | bytes 10616832 | tf_op jit(solution)/shard_map/dot_general | solution.py:51
  153.2 1.1 copy.43
  154.3 8.0 %all-to-all-start.2 = ((bf16[4,32,12,128]{3,0,2,1:T(4,128)(2,1)}), bf16[4,32,12,128]{3,0,2,1:T(4,128)(2,1)S(1)}, u32[]{:S(2)}, u32[]{:S(2)}) async-start(bf16[4,32,12,128]{3,0,2,1:T(4,128)(2,1)} %copy.43), calls=%async_computation.2 | async-start | bytes 786432 | tf_op jit(solution)/shard_map/all_to_all | solution.py:63
  162.8 0.5 fusion.16
  163.2 14.1 %all-to-all-done.2 = bf16[4,32,12,128]{3,0,2,1:T(4,128)(2,1)S(1)} async-done(((bf16[4,32,12,128]{3,0,2,1:T(4,128)(2,1)}), bf16[4,32,12,128]{3,0,2,1:T(4,128)(2,1)S(1)}, u32[]{:S(2)}, u32[]{:S(2)}) %all-to-all-start.2) | async-done | bytes 393248 | tf_op jit(solution)/shard_map/all_to_all | solution.py:63
  177.5 0.5 fusion.7
  178.0 1.5 fusion.4
  179.5 0.3 fusion.10
  179.9 1.2 copy.51
  181.1 4.7 %all-to-all-start.4 = ((bf16[128,1,12,128]{3,2,1,0:T(8,128)(2,1)}), bf16[128,1,12,128]{3,2,1,0:T(8,128)(2,1)S(1)}, u32[]{:S(2)}, u32[]{:S(2)}) async-start(bf16[128,1,12,128]{3,2,1,0:T(8,128)(2,1)} %copy.51), calls=%async_computation.4 | async-start | bytes 1048576 | tf_op jit(solution)/shard_map/all_to_all | solution.py:41
  185.8 0.4 fusion.9
  186.2 1.2 copy.54
  187.4 15.8 %all-to-all-done.4 = bf16[128,1,12,128]{3,2,1,0:T(8,128)(2,1)S(1)} async-done(((bf16[128,1,12,128]{3,2,1,0:T(8,128)(2,1)}), bf16[128,1,12,128]{3,2,1,0:T(8,128)(2,1)S(1)}, u32[]{:S(2)}, u32[]{:S(2)}) %all-to-all-start.4) | async-done | bytes 393248 | tf_op jit(solution)/shard_map/all_to_all | solution.py:41
  203.2 4.7 %all-to-all-start.5 = ((bf16[128,1,12,128]{3,2,1,0:T(8,128)(2,1)}), bf16[128,1,12,128]{3,2,1,0:T(8,128)(2,1)S(1)}, u32[]{:S(2)}, u32[]{:S(2)}) async-start(bf16[128,1,12,128]{3,2,1,0:T(8,128)(2,1)} %copy.54), calls=%async_computation.5 | async-start | bytes 1048576 | tf_op jit(solution)/shard_map/all_to_all | solution.py:42
  208.0 1.6 fusion.8
  209.5 1.2 copy.58
  210.7 14.8 %all-to-all-done.5 = bf16[128,1,12,128]{3,2,1,0:T(8,128)(2,1)S(1)} async-done(((bf16[128,1,12,128]{3,2,1,0:T(8,128)(2,1)}), bf16[128,1,12,128]{3,2,1,0:T(8,128)(2,1)S(1)}, u32[]{:S(2)}, u32[]{:S(2)}) %all-to-all-start.5) | async-done | bytes 393248 | tf_op jit(solution)/shard_map/all_to_all | solution.py:42
  225.5 4.7 %all-to-all-start.6 = ((bf16[128,1,12,128]{3,2,1,0:T(8,128)(2,1)}), bf16[128,1,12,128]{3,2,1,0:T(8,128)(2,1)S(1)}, u32[]{:S(2)}, u32[]{:S(2)}) async-start(bf16[128,1,12,128]{3,2,1,0:T(8,128)(2,1)} %copy.58), calls=%async_computation.6 | async-start | bytes 1048576 | tf_op jit(solution)/shard_map/all_to_all | solution.py:43
  230.4 0.8 copy.60
  231.3 0.8 copy.61
  232.1 15.7 %all-to-all-done.6 = bf16[128,1,12,128]{3,2,1,0:T(8,128)(2,1)S(1)} async-done(((bf16[128,1,12,128]{3,2,1,0:T(8,128)(2,1)}), bf16[128,1,12,128]{3,2,1,0:T(8,128)(2,1)S(1)}, u32[]{:S(2)}, u32[]{:S(2)}) %all-to-all-start.6) | async-done | bytes 393248 | tf_op jit(solution)/shard_map/all_to_all | solution.py:43
  247.9 0.8 copy.62
  (14 shorter events, 1.3 us)
Async XLA Ops:
  7.2 138.8 %copy-start = (bf16[4,32,3072]{2,1,0:T(8,128)(2,1)S(1)}, bf16[4,32,3072]{2,1,0:T(8,128)(2,1)}, u32[]{:S(2)}) copy-start(bf16[4,32,3072]{2,1,0:T(8,128)(2,1)} %param.8) | copy-start | bytes 2359300
  7.2 138.8 %all-gather.2.cloned.1.call-start = ((), (), s32[]{:S(2)}) async-start(), calls=%async_computation.7 | async-start | bytes 10027008 | tf_op jit(solution)/shard_map/all_gather | solution.py:53
  9.9 37.9 %all-to-all-start = ((bf16[4,32,12,128]{3,2,0,1:T(8,128)(2,1)}), bf16[4,32,12,128]{3,2,0,1:T(8,128)(2,1)S(1)}, u32[]{:S(2)}, u32[]{:S(2)}) async-start(bf16[4,32,12,128]{3,2,0,1:T(8,128)(2,1)} %copy.39), calls=%async_computation | async-start | bytes 1048576 | tf_op jit(solution)/shard_map/all_to_all | solution.py:60
  47.8 22.5 %all-to-all-start.1 = ((bf16[4,32,12,128]{3,2,0,1:T(8,128)(2,1)}), bf16[4,32,12,128]{3,2,0,1:T(8,128)(2,1)S(1)}, u32[]{:S(2)}, u32[]{:S(2)}) async-start(bf16[4,32,12,128]{3,2,0,1:T(8,128)(2,1)} %copy.41), calls=%async_computation.1 | async-start | bytes 1048576 | tf_op jit(solution)/shard_map/all_to_all | solution.py:61
  70.3 84.0 %all-to-all-start.3 = ((bf16[4,32,12,128]{3,2,0,1:T(8,128)(2,1)}), bf16[4,32,12,128]{3,2,0,1:T(8,128)(2,1)S(1)}, u32[]{:S(2)}, u32[]{:S(2)}) async-start(bf16[4,32,12,128]{3,2,0,1:T(8,128)(2,1)} %copy.45), calls=%async_computation.3 | async-start | bytes 1048576 | tf_op jit(solution)/shard_map/all_to_all | solution.py:62
  154.3 23.1 %all-to-all-start.2 = ((bf16[4,32,12,128]{3,0,2,1:T(4,128)(2,1)}), bf16[4,32,12,128]{3,0,2,1:T(4,128)(2,1)S(1)}, u32[]{:S(2)}, u32[]{:S(2)}) async-start(bf16[4,32,12,128]{3,0,2,1:T(4,128)(2,1)} %copy.43), calls=%async_computation.2 | async-start | bytes 786432 | tf_op jit(solution)/shard_map/all_to_all | solution.py:63
  163.2 14.7 %copy-start.1 = (f32[12,128,128]{1,2,0:T(8,128)}, f32[12,128,128]{1,2,0:T(8,128)S(1)}, u32[]{:S(2)}) copy-start(f32[12,128,128]{1,2,0:T(8,128)S(1)} %get-tuple-element.10) | copy-start | bytes 2359300
  181.1 22.2 %all-to-all-start.4 = ((bf16[128,1,12,128]{3,2,1,0:T(8,128)(2,1)}), bf16[128,1,12,128]{3,2,1,0:T(8,128)(2,1)S(1)}, u32[]{:S(2)}, u32[]{:S(2)}) async-start(bf16[128,1,12,128]{3,2,1,0:T(8,128)(2,1)} %copy.51), calls=%async_computation.4 | async-start | bytes 1048576 | tf_op jit(solution)/shard_map/all_to_all | solution.py:41
  203.2 22.3 %all-to-all-start.5 = ((bf16[128,1,12,128]{3,2,1,0:T(8,128)(2,1)}), bf16[128,1,12,128]{3,2,1,0:T(8,128)(2,1)S(1)}, u32[]{:S(2)}, u32[]{:S(2)}) async-start(bf16[128,1,12,128]{3,2,1,0:T(8,128)(2,1)} %copy.54), calls=%async_computation.5 | async-start | bytes 1048576 | tf_op jit(solution)/shard_map/all_to_all | solution.py:42
  225.5 22.3 %all-to-all-start.6 = ((bf16[128,1,12,128]{3,2,1,0:T(8,128)(2,1)}), bf16[128,1,12,128]{3,2,1,0:T(8,128)(2,1)S(1)}, u32[]{:S(2)}, u32[]{:S(2)}) async-start(bf16[128,1,12,128]{3,2,1,0:T(8,128)(2,1)} %copy.58), calls=%async_computation.6 | async-start | bytes 1048576 | tf_op jit(solution)/shard_map/all_to_all | solution.py:43
Sparse Core Ops, SparseCore 0:
  11.3 134.6 all-gather.1
where the time goes:
time: 257 us; the launch traced here: 256 us
  waiting for transfers between devices  169 us (66%)
  starting transfers between devices  46.3 us (18%)
  local copies, waits for them, and re-layouts  14.3 us (6%)
  between operations  14.2 us (6%)
  matrix products  11.7 us (5%)
    all_gather x1, waiting for transfers between devices, body(): lax.all_gather(out_proj, 'fsdp', axis=0, tiled=True)  71 us
    all_to_all x1, waiting for transfers between devices, body(): lax.all_to_all(queries, 'tm', split_axis=1, concat_axis=0, tiled=True)  22.8 us
    all_to_all x1, waiting for transfers between devices, send_back(): lax.all_to_all(grads[0], 'tm', split_axis=0, concat_axis=1, tiled=True)  15.8 us
    all_to_all x1, waiting for transfers between devices, send_back(): lax.all_to_all(grads[2], 'tm', split_axis=0, concat_axis=1, tiled=True)  15.7 us
    all_to_all x1, waiting for transfers between devices, send_back(): lax.all_to_all(grads[1], 'tm', split_axis=0, concat_axis=1, tiled=True)  14.8 us
    all_to_all x1, waiting for transfers between devices, body(): lax.all_to_all(key_states, 'tm', split_axis=1, concat_axis=0, tiled=True)  14.3 us
    all_to_all x1, waiting for transfers between devices, body(): lax.all_to_all(grad_attn, 'tm', split_axis=1, concat_axis=0, tiled=True)  14.1 us
    all_to_all x1, starting transfers between devices, body(): lax.all_to_all(queries, 'tm', split_axis=1, concat_axis=0, tiled=True)  13.2 us
  transfers between devices with their start and end apart: 8, of which 7 were waited for; matrix products, arithmetic and copies ran while one was open for 8% of the time, Pallas kernels for 0%

commit v1 on v0

--- a/solution.py
+++ b/solution.py
@@ -57,7 +57,12 @@
     grad_attn = grad_flat.reshape(frames_dev, pos_dev, heads, head_size)
     results = send_back(
         attend_back(
-            lax.all_to_all(queries, "tm", split_axis=1, concat_axis=0, tiled=True),
+            jnp.concatenate(
+                lax.all_to_all(
+                    jnp.stack(jnp.split(queries, lax.axis_size("tm"), axis=1)), "tm", 0, 0
+                ),
+                axis=0,
+            ),
             lax.all_to_all(key_states, "tm", split_axis=1, concat_axis=0, tiled=True),
             lax.all_to_all(value_states, "tm", split_axis=1, concat_axis=0, tiled=True),
             lax.all_to_all(grad_attn, "tm", split_axis=1, concat_axis=0, tiled=True),

time: 257 us -> 257 us (level)
  local copies, waits for them, and re-layouts: 14.3 us -> 36.2 us
  waiting for transfers between devices: 169 us -> 151 us
  starting transfers between devices: 46.3 us -> 42.1 us
    all_gather x1, waiting for transfers between devices: 71 us -> 3.7 us  [body(): lax.all_gather(out_proj, 'fsdp', axis=0, tiled=True)]
    all_to_all x1, waiting for transfers between devices: 14.3 us -> 65.8 us  [body(): lax.all_to_all(key_states, 'tm', split_axis=1, concat_axis=0, tiled=True)]
    unnamed x10 -> x39, local copies, waits for them, and re-layouts: 8.38 us -> 24.4 us
    all_to_all x1, waiting for transfers between devices: 22.8 us -> 14.8 us  [body(): lax.all_to_all(jnp.stack(jnp.split(queries, lax.axis_size('tm'), axis=1))...]
    all_to_all x1, waiting for transfers between devices: 0.01 us -> 5.04 us  [body(): lax.all_to_all(value_states, 'tm', split_axis=1, concat_axis=0, tiled=True)]
    split x0 -> x2, local copies, waits for them, and re-layouts: none -> 4.53 us  [body(): jnp.split(queries, lax.axis_size('tm'), axis=1)]
    all_to_all x1, starting transfers between devices: 8 us -> 5.09 us  [body(): lax.all_to_all(grad_attn, 'tm', split_axis=1, concat_axis=0, tiled=True)]
  transfers between devices with their start and end apart: 8 -> 8, of which waited for: 7 -> 8; matrix products, arithmetic and copies ran while one was open for 8% -> 17% of each run, Pallas kernels for 0% -> 0%
where the time goes in v1:
time: 257 us; the launch traced here: 256 us
  waiting for transfers between devices  151 us (59%)
  starting transfers between devices  42.1 us (16%)
  local copies, waits for them, and re-layouts  36.2 us (14%)
  between operations  14.2 us (6%)
  matrix products  12.5 us (5%)
    all_to_all x1, waiting for transfers between devices, body(): lax.all_to_all(key_states, 'tm', split_axis=1, concat_axis=0, tiled=True)  65.8 us
    unnamed x39, local copies, waits for them, and re-layouts  24.4 us
    all_to_all x1, waiting for transfers between devices, send_back(): lax.all_to_all(grads[0], 'tm', split_axis=0, concat_axis=1, tiled=True)  16.1 us
    all_to_all x1, waiting for transfers between devices, send_back(): lax.all_to_all(grads[1], 'tm', split_axis=0, concat_axis=1, tiled=True)  15.9 us
    all_to_all x1, waiting for transfers between devices, send_back(): lax.all_to_all(grads[2], 'tm', split_axis=0, concat_axis=1, tiled=True)  15.6 us
    all_to_all x1, waiting for transfers between devices, body(): lax.all_to_all(jnp.stack(jnp.split(queries, lax.axis_size('tm'), axis=1))...  14.8 us
    all_to_all x1, waiting for transfers between devices, body(): lax.all_to_all(grad_attn, 'tm', split_axis=1, concat_axis=0, tiled=True)  13.2 us
    all_to_all x1, starting transfers between devices, body(): lax.all_to_all(jnp.stack(jnp.split(queries, lax.axis_size('tm'), axis=1))...  13.2 us
  transfers between devices with their start and end apart: 8, of which 8 were waited for; matrix products, arithmetic and copies ran while one was open for 17% of the time, Pallas kernels for 0%

profile of v1, /device:TPU:64, one launch (start us, length us, event | category | flops | bytes accessed | tf_op | source)
XLA Modules:
  0.0 255.9 jit_solution(16892171481670234145)
XLA Ops:
  7.2 0.7 all-gather.2.cloned.1.call-update
  7.9 2.0 fusion.17
  17.2 2.5 fusion.16
  19.7 0.6 constant_dynamic-update-slice_fusion.19
  31.9 13.2 %all-to-all-start = ((bf16[32,4,1,12,128]{4,1,3,2,0:T(4,128)(2,1)}), bf16[32,4,1,12,128]{4,1,3,2,0:T(4,128)(2,1)S(1)}, u32[]{:S(2)}, u32[]{:S(2)}) async-start(bf16[32,4,1,12,128]{4,1,3,2,0:T(4,128)(2,1)} %constant_dynamic-update-slice_fusion), calls=%async_computation | async-start | bytes 786432 | tf_op jit(solution)/shard_map/all_to_all | solution.py:61
  45.0 2.0 copy.138
  47.0 14.8 %all-to-all-done = bf16[32,4,1,12,128]{4,1,3,2,0:T(4,128)(2,1)S(1)} async-done(((bf16[32,4,1,12,128]{4,1,3,2,0:T(4,128)(2,1)}), bf16[32,4,1,12,128]{4,1,3,2,0:T(4,128)(2,1)S(1)}, u32[]{:S(2)}, u32[]{:S(2)}) %all-to-all-start) | async-done | bytes 393248 | tf_op jit(solution)/shard_map/all_to_all | solution.py:61
  61.8 4.9 %all-to-all-start.1 = ((bf16[4,32,12,128]{3,2,0,1:T(8,128)(2,1)}), bf16[4,32,12,128]{3,2,0,1:T(8,128)(2,1)S(1)}, u32[]{:S(2)}, u32[]{:S(2)}) async-start(bf16[4,32,12,128]{3,2,0,1:T(8,128)(2,1)} %copy.138), calls=%async_computation.1 | async-start | bytes 1048576 | tf_op jit(solution)/shard_map/all_to_all | solution.py:66
  66.8 2.0 copy.142
  68.7 65.8 %all-to-all-done.1 = bf16[4,32,12,128]{3,2,0,1:T(8,128)(2,1)S(1)} async-done(((bf16[4,32,12,128]{3,2,0,1:T(8,128)(2,1)}), bf16[4,32,12,128]{3,2,0,1:T(8,128)(2,1)S(1)}, u32[]{:S(2)}, u32[]{:S(2)}) %all-to-all-start.1) | async-done | bytes 393248 | tf_op jit(solution)/shard_map/all_to_all | solution.py:66
  134.5 4.7 %all-to-all-start.3 = ((bf16[4,32,12,128]{3,2,0,1:T(8,128)(2,1)}), bf16[4,32,12,128]{3,2,0,1:T(8,128)(2,1)S(1)}, u32[]{:S(2)}, u32[]{:S(2)}) async-start(bf16[4,32,12,128]{3,2,0,1:T(8,128)(2,1)} %copy.142), calls=%async_computation.3 | async-start | bytes 1048576 | tf_op jit(solution)/shard_map/all_to_all | solution.py:67
  139.3 3.7 %all-gather.2.cloned.1.call-done = bf16[1536,3072]{1,0:T(8,128)(2,1)} async-done(((bf16[96,3072]{1,0:T(8,128)(2,1)}), bf16[1536,3072]{1,0:T(8,128)(2,1)}) %all-gather.2.cloned.1.call-update) | async-done | bytes 9437200 | tf_op jit(solution)/shard_map/all_gather | solution.py:53
  143.0 6.9 %convolution_convert_fusion = bf16[128,1536]{1,0:T(8,128)(2,1)S(1)} fusion(bf16[128,3072]{1,0:T(8,128)(2,1)S(1)} %bitcast.193, bf16[1536,3072]{1,0:T(8,128)(2,1)} %all-gather.2.cloned.1.call-done), kind=kOutput, calls=%fused_computation.1 | convolution fusion | flops 1208156160 | bytes 10616832 | tf_op jit(solution)/shard_map/dot_general | solution.py:51
  150.2 1.1 copy.140
  151.2 5.0 %all-to-all-done.3 = bf16[4,32,12,128]{3,2,0,1:T(8,128)(2,1)S(1)} async-done(((bf16[4,32,12,128]{3,2,0,1:T(8,128)(2,1)}), bf16[4,32,12,128]{3,2,0,1:T(8,128)(2,1)S(1)}, u32[]{:S(2)}, u32[]{:S(2)}) %all-to-all-start.3) | async-done | bytes 393248 | tf_op jit(solution)/shard_map/all_to_all | solution.py:67
  156.3 5.1 %all-to-all-start.2 = ((bf16[4,32,12,128]{3,0,2,1:T(4,128)(2,1)}), bf16[4,32,12,128]{3,0,2,1:T(4,128)(2,1)S(1)}, u32[]{:S(2)}, u32[]{:S(2)}) async-start(bf16[4,32,12,128]{3,0,2,1:T(4,128)(2,1)} %copy.140), calls=%async_computation.2 | async-start | bytes 786432 | tf_op jit(solution)/shard_map/all_to_all | solution.py:68
  161.9 1.4 fusion.18
  163.2 13.2 %all-to-all-done.2 = bf16[4,32,12,128]{3,0,2,1:T(4,128)(2,1)S(1)} async-done(((bf16[4,32,12,128]{3,0,2,1:T(4,128)(2,1)}), bf16[4,32,12,128]{3,0,2,1:T(4,128)(2,1)S(1)}, u32[]{:S(2)}, u32[]{:S(2)}) %all-to-all-start.2) | async-done | bytes 393248 | tf_op jit(solution)/shard_map/all_to_all | solution.py:68
  176.6 1.7 fusion.7
  178.3 1.5 fusion.4
  180.2 1.2 copy.148
  181.4 4.7 %all-to-all-start.4 = ((bf16[128,1,12,128]{3,2,1,0:T(8,128)(2,1)}), bf16[128,1,12,128]{3,2,1,0:T(8,128)(2,1)S(1)}, u32[]{:S(2)}, u32[]{:S(2)}) async-start(bf16[128,1,12,128]{3,2,1,0:T(8,128)(2,1)} %copy.148), calls=%async_computation.4 | async-start | bytes 1048576 | tf_op jit(solution)/shard_map/all_to_all | solution.py:41
  186.3 1.1 copy.153
  187.4 16.1 %all-to-all-done.4 = bf16[128,1,12,128]{3,2,1,0:T(8,128)(2,1)S(1)} async-done(((bf16[128,1,12,128]{3,2,1,0:T(8,128)(2,1)}), bf16[128,1,12,128]{3,2,1,0:T(8,128)(2,1)S(1)}, u32[]{:S(2)}, u32[]{:S(2)}) %all-to-all-start.4) | async-done | bytes 393248 | tf_op jit(solution)/shard_map/all_to_all | solution.py:41
  203.6 4.7 %all-to-all-start.5 = ((bf16[128,1,12,128]{3,2,1,0:T(8,128)(2,1)}), bf16[128,1,12,128]{3,2,1,0:T(8,128)(2,1)S(1)}, u32[]{:S(2)}, u32[]{:S(2)}) async-start(bf16[128,1,12,128]{3,2,1,0:T(8,128)(2,1)} %copy.153), calls=%async_computation.5 | async-start | bytes 1048576 | tf_op jit(solution)/shard_map/all_to_all | solution.py:42
  208.7 1.2 copy.157
  209.9 15.9 %all-to-all-done.5 = bf16[128,1,12,128]{3,2,1,0:T(8,128)(2,1)S(1)} async-done(((bf16[128,1,12,128]{3,2,1,0:T(8,128)(2,1)}), bf16[128,1,12,128]{3,2,1,0:T(8,128)(2,1)S(1)}, u32[]{:S(2)}, u32[]{:S(2)}) %all-to-all-start.5) | async-done | bytes 393248 | tf_op jit(solution)/shard_map/all_to_all | solution.py:42
  225.8 4.7 %all-to-all-start.6 = ((bf16[128,1,12,128]{3,2,1,0:T(8,128)(2,1)}), bf16[128,1,12,128]{3,2,1,0:T(8,128)(2,1)S(1)}, u32[]{:S(2)}, u32[]{:S(2)}) async-start(bf16[128,1,12,128]{3,2,1,0:T(8,128)(2,1)} %copy.157), calls=%async_computation.6 | async-start | bytes 1048576 | tf_op jit(solution)/shard_map/all_to_all | solution.py:43
  230.7 0.8 copy.159
  231.5 1.0 copy.303
  232.5 15.6 %all-to-all-done.6 = bf16[128,1,12,128]{3,2,1,0:T(8,128)(2,1)S(1)} async-done(((bf16[128,1,12,128]{3,2,1,0:T(8,128)(2,1)}), bf16[128,1,12,128]{3,2,1,0:T(8,128)(2,1)S(1)}, u32[]{:S(2)}, u32[]{:S(2)}) %all-to-all-start.6) | async-done | bytes 393248 | tf_op jit(solution)/shard_map/all_to_all | solution.py:43
  248.2 0.8 copy.160
  (46 shorter events, 21.0 us)
Async XLA Ops:
  7.2 135.8 %copy-start = (bf16[4,32,3072]{2,1,0:T(8,128)(2,1)S(1)}, bf16[4,32,3072]{2,1,0:T(8,128)(2,1)}, u32[]{:S(2)}) copy-start(bf16[4,32,3072]{2,1,0:T(8,128)(2,1)} %param.8) | copy-start | bytes 2359300
  7.2 135.8 %all-gather.2.cloned.1.call-start = ((), (), s32[]{:S(2)}) async-start(), calls=%async_computation.7 | async-start | bytes 10027008 | tf_op jit(solution)/shard_map/all_gather | solution.py:53
  31.9 30.0 %all-to-all-start = ((bf16[32,4,1,12,128]{4,1,3,2,0:T(4,128)(2,1)}), bf16[32,4,1,12,128]{4,1,3,2,0:T(4,128)(2,1)S(1)}, u32[]{:S(2)}, u32[]{:S(2)}) async-start(bf16[32,4,1,12,128]{4,1,3,2,0:T(4,128)(2,1)} %constant_dynamic-update-slice_fusion), calls=%async_computation | async-start | bytes 786432 | tf_op jit(solution)/shard_map/all_to_all | solution.py:61
  61.8 72.7 %all-to-all-start.1 = ((bf16[4,32,12,128]{3,2,0,1:T(8,128)(2,1)}), bf16[4,32,12,128]{3,2,0,1:T(8,128)(2,1)S(1)}, u32[]{:S(2)}, u32[]{:S(2)}) async-start(bf16[4,32,12,128]{3,2,0,1:T(8,128)(2,1)} %copy.138), calls=%async_computation.1 | async-start | bytes 1048576 | tf_op jit(solution)/shard_map/all_to_all | solution.py:66
  134.5 21.7 %all-to-all-start.3 = ((bf16[4,32,12,128]{3,2,0,1:T(8,128)(2,1)}), bf16[4,32,12,128]{3,2,0,1:T(8,128)(2,1)S(1)}, u32[]{:S(2)}, u32[]{:S(2)}) async-start(bf16[4,32,12,128]{3,2,0,1:T(8,128)(2,1)} %copy.142), calls=%async_computation.3 | async-start | bytes 1048576 | tf_op jit(solution)/shard_map/all_to_all | solution.py:67
  156.3 20.2 %all-to-all-start.2 = ((bf16[4,32,12,128]{3,0,2,1:T(4,128)(2,1)}), bf16[4,32,12,128]{3,0,2,1:T(4,128)(2,1)S(1)}, u32[]{:S(2)}, u32[]{:S(2)}) async-start(bf16[4,32,12,128]{3,0,2,1:T(4,128)(2,1)} %copy.140), calls=%async_computation.2 | async-start | bytes 786432 | tf_op jit(solution)/shard_map/all_to_all | solution.py:68
  176.6 31.7 %copy-start.1 = (f32[12,128,128]{1,2,0:T(8,128)S(1)}, f32[12,128,128]{1,2,0:T(8,128)}, u32[]{:S(2)}) copy-start(f32[12,128,128]{1,2,0:T(8,128)} %get-tuple-element.42) | copy-start | bytes 2359300
  181.4 22.2 %all-to-all-start.4 = ((bf16[128,1,12,128]{3,2,1,0:T(8,128)(2,1)}), bf16[128,1,12,128]{3,2,1,0:T(8,128)(2,1)S(1)}, u32[]{:S(2)}, u32[]{:S(2)}) async-start(bf16[128,1,12,128]{3,2,1,0:T(8,128)(2,1)} %copy.148), calls=%async_computation.4 | async-start | bytes 1048576 | tf_op jit(solution)/shard_map/all_to_all | solution.py:41
  203.6 22.3 %all-to-all-start.5 = ((bf16[128,1,12,128]{3,2,1,0:T(8,128)(2,1)}), bf16[128,1,12,128]{3,2,1,0:T(8,128)(2,1)S(1)}, u32[]{:S(2)}, u32[]{:S(2)}) async-start(bf16[128,1,12,128]{3,2,1,0:T(8,128)(2,1)} %copy.153), calls=%async_computation.5 | async-start | bytes 1048576 | tf_op jit(solution)/shard_map/all_to_all | solution.py:42
  225.8 22.3 %all-to-all-start.6 = ((bf16[128,1,12,128]{3,2,1,0:T(8,128)(2,1)}), bf16[128,1,12,128]{3,2,1,0:T(8,128)(2,1)S(1)}, u32[]{:S(2)}, u32[]{:S(2)}) async-start(bf16[128,1,12,128]{3,2,1,0:T(8,128)(2,1)} %copy.157), calls=%async_computation.6 | async-start | bytes 1048576 | tf_op jit(solution)/shard_map/all_to_all | solution.py:43
Sparse Core Ops, SparseCore 0:
  11.3 131.6 all-gather.1
